TPU v7x, 512 devices: a whole 4x4x16 slice. The times are simulated.
512 devices in a mesh: segment: 4 (over x), expert: 64 (over y, z), dp: 2 (over core).
Axes of the slice: x: 4, y: 4, z: 16, core: 2. Of those that a mesh axis runs over, the one named last changes fastest.
Arguments:
- act_in: bfloat16 [4, 14336, 2048], P('segment', ('expert', 'dp')), may hold values from -6 to 6
- stash_in: bfloat16 [4, 14336, 2048], P('segment', ('expert', 'dp')), may hold values from -6 to 6
- grad_in: bfloat16 [4, 14336, 2048], P('segment', ('expert', 'dp')), may hold values from -6 to 6
- route_a: int32 [4, 14336, 2], P('segment', ('expert', 'dp')), may hold values from 0 to 31, all different within a row; in each aligned block of 112 rows (0 to 111, 112 to 223, ..., all dimensions but the last counted through in order) at most 8 rows name the same one
- route_b: int32 [4, 14336, 2], P('segment', ('expert', 'dp')), may hold values from 0 to 31, all different within a row; in each aligned block of 112 rows (0 to 111, 112 to 223, ..., all dimensions but the last counted through in order) at most 8 rows name the same one
- norm_gain: float32 [4, 2048], P('segment'), may hold values from 0.5 to 1.5
- router: bfloat16 [4, 32, 2048], P('segment'), may hold values from -0.5 to 0.5
- gate_weight: bfloat16 [4, 64, 352, 2048], P('segment', 'expert', 'dp'), may hold values from -0.125 to 0.125
- up_weight: bfloat16 [4, 64, 352, 2048], P('segment', 'expert', 'dp'), may hold values from -0.125 to 0.125
- down_weight: bfloat16 [4, 64, 352, 2048], P('segment', 'expert', 'dp'), may hold values from -0.21875 to 0.21875
Outputs:
- next_act: bfloat16 [4, 14336, 2048], P('segment', ('expert', 'dp'))
- prev_grad: bfloat16 [4, 14336, 2048], P('segment', ('expert', 'dp'))
- router_grad: float32 [4, 32, 2048], P('segment')
- gain_grad: float32 [4, 2048], P('segment')
Inputs may be any that keep to these rules, and one draw needn't show every extreme that they name: `route_a`: each row names two different experts. In each aligned block of 112 rows (the tokens of one device) no expert is named more than 8 times, a bound that some block reaches in every draw. `route_b`: as route_a.
All inputs are finite; a program needn't handle non-finite values.
Results may differ from a plain program's by a relative error of at most 0.011.
Values may be sent and summed in bfloat16 or wider, within the bound.
A program may use at most 64 MiB of HBM per device.

v0:
```python
import jax
import jax.numpy as jnp
from jax import lax
from jax.sharding import PartitionSpec as P

EPS = 1e-06


def partner_2(shard, axis, stride):
    return lax.ppermute(shard, axis, [(i, i ^ 1 << stride) for i in range(lax.axis_size(axis))])


def from_behind(value, axis, steps):
    count = lax.axis_size(axis)
    pairs = [(source, (source + steps) % count) for source in range(count)]
    return lax.ppermute(value, axis, pairs)


def order_halves(own_part, far_part, parity):
    low_half = jnp.where(parity == 0, own_part, far_part)
    high_half = jnp.where(parity == 0, far_part, own_part)
    return jnp.stack([low_half, high_half])


def prepare(x_block, route, gain, router_w):
    x_float = x_block.astype(jnp.float32)
    inv_rms = lax.rsqrt(jnp.mean(x_float * x_float, -1, keepdims=True) + EPS)
    normed = (x_float * inv_rms * gain[None, :]).astype(jnp.bfloat16)
    logits = jnp.einsum("td,ed->te", normed, router_w, preferred_element_type=jnp.float32)
    chosen_mask = route[:, :, None] == jnp.arange(router_w.shape[0], dtype=jnp.int32)[None, None, :]
    chosen = jnp.sum(jnp.where(chosen_mask, logits[:, None, :], 0.0), -1)
    weight_one = jax.nn.sigmoid(chosen[:, 0] - chosen[:, 1])
    weight_two = jax.nn.sigmoid(chosen[:, 1] - chosen[:, 0])
    return (x_float, inv_rms, normed, chosen_mask, weight_one, weight_two)


def route_slots(route, experts, capacity, owners, offset):
    expert_ids = route.reshape(-1)
    onehot = (expert_ids[:, None] == jnp.arange(experts, dtype=jnp.int32)[None, :]).astype(
        jnp.int32
    )
    rank = jnp.sum(jnp.cumsum(onehot, axis=0) * onehot, -1) - 1
    position = (2 * expert_ids + (rank + offset) % 2) * capacity + rank // 2
    pair_count = expert_ids.shape[0]
    slot_pair = jnp.full((owners * capacity,), pair_count, jnp.int32)
    slot_pair = slot_pair.at[position].set(jnp.arange(pair_count, dtype=jnp.int32))
    return (position, slot_pair)


def pad_rows(rows):
    return jnp.concatenate([rows, jnp.zeros((1, rows.shape[1]), rows.dtype)], 0)


def body(
    act_in,
    stash_in,
    grad_in,
    route_a,
    route_b,
    norm_gain,
    router,
    gate_weight,
    up_weight,
    down_weight,
):
    parity = lax.axis_index("expert") % 2
    quarters = (gate_weight[0, 0], up_weight[0, 0], down_weight[0, 0])
    halves = (
        lax.all_gather(quarters[0], "dp", axis=0, tiled=True),
        lax.all_gather(quarters[1], "dp", axis=0, tiled=True),
        lax.all_gather(quarters[2], "dp", axis=0, tiled=True),
    )
    partner = partner_2((halves[0], halves[1], halves[2]), "expert", 0)
    weights = tuple((order_halves(halves[which], partner[which], parity) for which in range(3)))
    gate_full, up_full, down_full = weights
    gain = norm_gain[0]
    router_w = router[0]
    experts = router_w.shape[0]
    width = act_in.shape[2]
    tokens = act_in.shape[1]
    owners = lax.axis_size("expert")
    most_rows = 2 * min(tokens // experts + 1, tokens // 2)
    capacity = (most_rows + 1) // 2

    def expert_forward(block_rows):
        flat_rows = block_rows.reshape(-1, width)
        gate_val = jnp.einsum(
            "rd,phd->rph", flat_rows, gate_full, preferred_element_type=jnp.float32
        )
        up_val = jnp.einsum("rd,phd->rph", flat_rows, up_full, preferred_element_type=jnp.float32)
        hidden = (jax.nn.silu(gate_val) * up_val).astype(jnp.bfloat16)
        output = jnp.einsum("rph,phd->rd", hidden, down_full, preferred_element_type=jnp.float32)
        return (output.astype(jnp.bfloat16).reshape(block_rows.shape), gate_val, up_val)

    x_float, inv_rms, normed, chosen_mask, weight_one, weight_two = prepare(
        act_in[0], route_a[0], gain, router_w
    )
    position, slot_pair = route_slots(route_a[0], experts, capacity, owners, parity)
    send_rows = jnp.take(pad_rows(normed), slot_pair // 2, axis=0).reshape(owners, capacity, width)
    output, gate_val, up_val = expert_forward(
        lax.all_to_all(send_rows, "expert", split_axis=0, concat_axis=0, tiled=True)
    )
    returned = lax.all_to_all(output, "expert", split_axis=0, concat_axis=0, tiled=True)
    pair_out = (
        jnp.take(returned.reshape(-1, width), position, axis=0)
        .reshape(tokens, 2, width)
        .astype(jnp.float32)
    )
    mixed = x_float + weight_one[:, None] * pair_out[:, 0] + weight_two[:, None] * pair_out[:, 1]
    next_act = from_behind(mixed.astype(jnp.bfloat16), "segment", 1)
    x_float, inv_rms, normed, chosen_mask, weight_one, weight_two = prepare(
        stash_in[0], route_b[0], gain, router_w
    )
    position, slot_pair = route_slots(route_b[0], experts, capacity, owners, parity)
    send_rows = jnp.take(pad_rows(normed), slot_pair // 2, axis=0).reshape(owners, capacity, width)
    received = lax.all_to_all(send_rows, "expert", split_axis=0, concat_axis=0, tiled=True)
    expert_out, gate_val, up_val = expert_forward(received)
    returned = lax.all_to_all(expert_out, "expert", split_axis=0, concat_axis=0, tiled=True)
    pair_out = (
        jnp.take(returned.reshape(-1, width), position, axis=0)
        .reshape(tokens, 2, width)
        .astype(jnp.float32)
    )
    out_grad = grad_in[0].astype(jnp.float32)
    dot_one = jnp.sum(out_grad * pair_out[:, 0], -1)
    dot_two = jnp.sum(out_grad * pair_out[:, 1], -1)
    logit_grad = weight_one * weight_two * (dot_one - dot_two)
    signs = chosen_mask[:, 0].astype(jnp.float32) - chosen_mask[:, 1].astype(jnp.float32)
    dlogits = (logit_grad[:, None] * signs).astype(jnp.bfloat16)
    pair_grad = jnp.stack(
        [weight_one[:, None] * out_grad, weight_two[:, None] * out_grad], 1
    ).astype(jnp.bfloat16)
    send_grads = jnp.take(
        pad_rows(pair_grad.reshape(tokens * 2, width)), slot_pair, axis=0
    ).reshape(owners, capacity, width)
    grad_rows = lax.all_to_all(
        send_grads, "expert", split_axis=0, concat_axis=0, tiled=True
    ).reshape(-1, width)
    grad_hidden = jnp.einsum(
        "rd,phd->rph", grad_rows, down_full, preferred_element_type=jnp.float32
    )
    sigma = jax.nn.sigmoid(gate_val)
    grad_gate = (grad_hidden * up_val * sigma * (1.0 + gate_val * (1.0 - sigma))).astype(
        jnp.bfloat16
    )
    grad_up = (grad_hidden * gate_val * sigma).astype(jnp.bfloat16)
    grad_normed_rows = jnp.einsum(
        "rph,phd->rd", grad_gate, gate_full, preferred_element_type=jnp.float32
    )
    grad_normed_rows = grad_normed_rows + jnp.einsum(
        "rph,phd->rd", grad_up, up_full, preferred_element_type=jnp.float32
    )
    grad_normed_rows = grad_normed_rows.astype(jnp.bfloat16).reshape(owners, capacity, width)
    grad_back = lax.all_to_all(grad_normed_rows, "expert", split_axis=0, concat_axis=0, tiled=True)
    pair_back = (
        jnp.take(grad_back.reshape(-1, width), position, axis=0)
        .reshape(tokens, 2, width)
        .astype(jnp.float32)
    )
    dnormed = (
        pair_back[:, 0]
        + pair_back[:, 1]
        + jnp.dot(dlogits, router_w, preferred_element_type=jnp.float32)
    )
    router_term = jnp.einsum("te,td->ed", dlogits, normed, preferred_element_type=jnp.float32)
    gain_term = jnp.sum(dnormed * x_float * inv_rms, 0)
    router_sum, gain_sum = lax.psum((router_term, gain_term), ("expert", "dp"))
    blocks = lax.axis_size("expert") * lax.axis_size("dp")
    dxn = dnormed * gain[None, :]
    input_grad = (
        out_grad + inv_rms * dxn - x_float * inv_rms**3 * jnp.mean(dxn * x_float, -1, keepdims=True)
    )
    prev_grad = from_behind(input_grad.astype(jnp.bfloat16), "segment", -1)
    return (next_act[None], prev_grad[None], (router_sum / blocks)[None], (gain_sum / blocks)[None])


def solution(mesh):
    in_specs = (
        P("segment", ("expert", "dp"), None),
        P("segment", ("expert", "dp"), None),
        P("segment", ("expert", "dp"), None),
        P("segment", ("expert", "dp"), None),
        P("segment", ("expert", "dp"), None),
        P("segment", None),
        P("segment", None, None),
        P("segment", "expert", "dp", None),
        P("segment", "expert", "dp", None),
        P("segment", "expert", "dp", None),
    )
    out_specs = (
        P("segment", ("expert", "dp"), None),
        P("segment", ("expert", "dp"), None),
        P("segment", None, None),
        P("segment", None),
    )
    return jax.shard_map(body, mesh=mesh, in_specs=in_specs, out_specs=out_specs, check_vma=False)
```

profile of v0, /device:TPU:1, one launch (start us, length us, event | category | flops | bytes accessed | tf_op | source)
XLA Modules:
  0.0 1096.4 jit_solution(4540719086788931568)
XLA Ops:
  16.1 1.3 scatter_custom_fusion.1
  17.4 1.4 gather_fusion.3
  19.0 1.3 reshape.523
  20.2 19.3 %all-to-all-start.3 = ((bf16[64,4,2048]{2,1,0:T(4,128)(2,1)}), bf16[64,4,2048]{2,1,0:T(4,128)(2,1)S(1)}, u32[]{:S(2)}, u32[]{:S(2)}) async-start(bf16[64,4,2048]{2,1,0:T(4,128)(2,1)} %reshape.523), calls=%async_computation.3 | async-start | bytes 2097152 | tf_op jit(solution)/shard_map/all_to_all | solution.py:116
  40.3 2.9 collective-permute-start
  43.2 17.3 %all-gather.9.cloned.1.call-done = bf16[1,1,352,2048]{3,2,1,0:T(8,128)(2,1)} async-done(((bf16[1,1,176,2048]{3,2,1,0:T(8,128)(2,1)}), bf16[1,1,352,2048]{3,2,1,0:T(8,128)(2,1)}) %all-gather.9.cloned.1.call-update) | async-done | bytes 1441808 | tf_op jit(solution)/shard_map/all_gather | solution.py:70
  60.5 2.2 collective-permute-start.1
  62.7 21.4 %all-gather.11.cloned.1.call-done = bf16[1,1,352,2048]{3,2,1,0:T(8,128)(2,1)} async-done(((bf16[1,1,176,2048]{3,2,1,0:T(8,128)(2,1)}), bf16[1,1,352,2048]{3,2,1,0:T(8,128)(2,1)}) %all-gather.11.cloned.1.call-update) | async-done | bytes 1441808 | tf_op jit(solution)/shard_map/all_gather | solution.py:71
  84.1 2.2 collective-permute-start.2
  86.3 30.3 %collective-permute-done = bf16[352,2048]{1,0:T(8,128)(2,1)} collective-permute-done((bf16[352,2048]{1,0:T(8,128)(2,1)}, bf16[352,2048]{1,0:T(8,128)(2,1)}, u32[]{:S(2)}, u32[]{:S(2)}) %collective-permute-start) | collective-permute-done | bytes 1441824 | tf_op jit(solution)/shard_map/ppermute | solution.py:10
  116.5 3.1 select_bitcast_fusion.5
  119.6 27.8 %collective-permute-done.1 = bf16[352,2048]{1,0:T(8,128)(2,1)} collective-permute-done((bf16[352,2048]{1,0:T(8,128)(2,1)}, bf16[352,2048]{1,0:T(8,128)(2,1)}, u32[]{:S(2)}, u32[]{:S(2)}) %collective-permute-start.1) | collective-permute-done | bytes 1441824 | tf_op jit(solution)/shard_map/ppermute | solution.py:10
  147.4 3.2 select_bitcast_fusion.3
  150.6 27.7 %collective-permute-done.2 = bf16[352,2048]{1,0:T(8,128)(2,1)} collective-permute-done((bf16[352,2048]{1,0:T(8,128)(2,1)}, bf16[352,2048]{1,0:T(8,128)(2,1)}, u32[]{:S(2)}, u32[]{:S(2)}) %collective-permute-start.2) | collective-permute-done | bytes 1441824 | tf_op jit(solution)/shard_map/ppermute | solution.py:10
  178.3 3.2 select_bitcast_fusion.1
  182.6 2.8 fusion.45
  190.1 15.0 %all-to-all-start.5 = ((bf16[64,4,2048]{2,1,0:T(4,128)(2,1)}), bf16[64,4,2048]{2,1,0:T(4,128)(2,1)S(1)}, u32[]{:S(2)}, u32[]{:S(2)}) async-start(bf16[64,4,2048]{2,1,0:T(4,128)(2,1)} %reshape.527), calls=%async_computation.5 | async-start | bytes 2097152 | tf_op jit(solution)/shard_map/all_to_all | solution.py:118
  205.7 49.7 %all-to-all-done.5 = bf16[64,4,2048]{2,1,0:T(4,128)(2,1)S(1)} async-done(((bf16[64,4,2048]{2,1,0:T(4,128)(2,1)}), bf16[64,4,2048]{2,1,0:T(4,128)(2,1)S(1)}, u32[]{:S(2)}, u32[]{:S(2)}) %all-to-all-start.5) | async-done | bytes 1048608 | tf_op jit(solution)/shard_map/all_to_all | solution.py:118
  255.7 1.3 gather_fusion.5
  256.9 1.4 select_convert_fusion
  258.3 2.4 reshape.537
  260.7 1.4 fusion.96
  265.0 1.4 gather_fusion
  267.4 60.5 %all_to_all.30 = bf16[64,4,2048]{2,1,0:T(4,128)(2,1)S(1)} all-to-all(bf16[64,4,2048]{2,1,0:T(4,128)(2,1)S(1)} %broadcast_select_fusion.2), channel_id=1, replica_groups=mesh['segment'=4,'expert'=64,'dp'=2] {'expert'}, dimensions={0} | all-to-all | bytes 2097152 | tf_op jit(solution)/shard_map/all_to_all | solution.py:136
  329.0 2.8 fusion.42
  335.0 1.3 reshape.525
  336.2 10.1 all-to-all-start.4
  346.4 1.4 scatter_custom_fusion
  347.8 48.8 %all-to-all-done.4 = bf16[64,4,2048]{2,1,0:T(4,128)(2,1)S(1)} async-done(((bf16[64,4,2048]{2,1,0:T(4,128)(2,1)}), bf16[64,4,2048]{2,1,0:T(4,128)(2,1)S(1)}, u32[]{:S(2)}, u32[]{:S(2)}) %all-to-all-start.4) | async-done | bytes 1048608 | tf_op jit(solution)/shard_map/all_to_all | solution.py:154
  398.2 1.5 select_convert_fusion.1
  399.7 2.4 reshape.536
  402.1 1.4 fusion.95
  405.9 1.4 gather_fusion.1
  407.8 60.2 %all_to_all.31 = bf16[64,4,2048]{2,1,0:T(4,128)(2,1)S(1)} all-to-all(bf16[64,4,2048]{2,1,0:T(4,128)(2,1)S(1)} %reshape.516), channel_id=1, replica_groups=mesh['segment'=4,'expert'=64,'dp'=2] {'expert'}, dimensions={0} | all-to-all | bytes 2097152 | tf_op jit(solution)/shard_map/all_to_all | solution.py:101
  469.2 4.0 fusion.44
  473.3 7.1 fusion.2
  480.3 2.2 reshape.518
  482.6 10.2 all-to-all-start.1
  494.4 4.4 collective-permute-start.4
  498.8 44.7 %all-to-all-done.1 = bf16[64,4,2048]{2,1,0:T(4,128)(2,1)S(1)} async-done(((bf16[64,4,2048]{2,1,0:T(4,128)(2,1)}), bf16[64,4,2048]{2,1,0:T(4,128)(2,1)S(1)}, u32[]{:S(2)}, u32[]{:S(2)}) %all-to-all-start.1) | async-done | bytes 1048608 | tf_op jit(solution)/shard_map/all_to_all | solution.py:103
  545.0 1.5 select_convert_fusion.2
  546.5 2.4 reshape.531
  548.9 1.4 fusion.97
  551.2 3.1 collective-permute-start.3
  554.4 278.7 %all-reduce.7.cloned.1.call-done = f32[32,2048]{1,0:T(8,128)} async-done(((f32[32,2048]{1,0:T(8,128)}), f32[32,2048]{1,0:T(8,128)}) %all-reduce.7.cloned.1.call-update) | async-done | bytes 262160 | tf_op jit(solution)/shard_map/psum | solution.py:167
  833.1 1.7 multiply_bitcast_fusion
  834.8 251.6 %psum.15 = f32[2048]{0:T(1024)S(1)} all-reduce(f32[2048]{0:T(1024)S(1)} %get-tuple-element.6), channel_id=1, replica_groups=mesh['segment'=4,'expert'=64,'dp'=2] {'expert','dp'}, use_global_device_ids=true, to_apply=%region_17.20 | all-reduce | flops 2048 | bytes 16384 | tf_op jit(solution)/shard_map/psum | solution.py:167
  1087.8 1.8 copy.74
  (156 shorter events, 35.1 us)
Async XLA Ops:
  7.2 198.1 %copy-start = (bf16[1,32,2048]{2,1,0:T(8,128)(2,1)S(1)}, bf16[1,32,2048]{2,1,0:T(8,128)(2,1)}, u32[]{:S(2)}) copy-start(bf16[1,32,2048]{2,1,0:T(8,128)(2,1)} %param.20) | copy-start | bytes 393220
  7.2 7.2 copy-start.2
  7.2 7.4 copy-start.1
  7.2 8.1 copy-start.20
  7.2 33.0 %all-gather.7.cloned.1.call-start = ((), (), s32[]{:S(2)}) async-start(), calls=%async_computation.7 | async-start | bytes 2162688 | tf_op jit(solution)/shard_map/all_gather | solution.py:69
  7.9 52.6 %all-gather.9.cloned.1.call-start = ((), (), s32[]{:S(2)}) async-start(), calls=%async_computation.8 | async-start | bytes 2162688 | tf_op jit(solution)/shard_map/all_gather | solution.py:70
  20.2 161.3 %all-to-all-start.3 = ((bf16[64,4,2048]{2,1,0:T(4,128)(2,1)}), bf16[64,4,2048]{2,1,0:T(4,128)(2,1)S(1)}, u32[]{:S(2)}, u32[]{:S(2)}) async-start(bf16[64,4,2048]{2,1,0:T(4,128)(2,1)} %reshape.523), calls=%async_computation.3 | async-start | bytes 2097152 | tf_op jit(solution)/shard_map/all_to_all | solution.py:116
  39.5 44.6 %all-gather.11.cloned.1.call-start = ((), (), s32[]{:S(2)}) async-start(), calls=%async_computation.9 | async-start | bytes 2162688 | tf_op jit(solution)/shard_map/all_gather | solution.py:71
  40.3 76.3 %collective-permute-start = (bf16[352,2048]{1,0:T(8,128)(2,1)}, bf16[352,2048]{1,0:T(8,128)(2,1)}, u32[]{:S(2)}, u32[]{:S(2)}) collective-permute-start(bf16[352,2048]{1,0:T(8,128)(2,1)} %bitcast.208), channel_id=1, source_target_pairs={{0,2},{2,0},{4,6},{6,4},{8,10},{10,8},{12,14},{14,12},{16,18},{18,... | collective-permute-start | bytes 4325384 | tf_op jit(solution)/shard_map/ppermute | solution.py:10
  60.5 86.9 %collective-permute-start.1 = (bf16[352,2048]{1,0:T(8,128)(2,1)}, bf16[352,2048]{1,0:T(8,128)(2,1)}, u32[]{:S(2)}, u32[]{:S(2)}) collective-permute-start(bf16[352,2048]{1,0:T(8,128)(2,1)} %bitcast.209), channel_id=1, source_target_pairs={{0,2},{2,0},{4,6},{6,4},{8,10},{10,8},{12,14},{14,12},{16,18},{18,... | collective-permute-start | bytes 4325384 | tf_op jit(solution)/shard_map/ppermute | solution.py:10
  84.1 94.3 %collective-permute-start.2 = (bf16[352,2048]{1,0:T(8,128)(2,1)}, bf16[352,2048]{1,0:T(8,128)(2,1)}, u32[]{:S(2)}, u32[]{:S(2)}) collective-permute-start(bf16[352,2048]{1,0:T(8,128)(2,1)} %bitcast.210), channel_id=1, source_target_pairs={{0,2},{2,0},{4,6},{6,4},{8,10},{10,8},{12,14},{14,12},{16,18},{18,... | collective-permute-start | bytes 4325384 | tf_op jit(solution)/shard_map/ppermute | solution.py:10
  86.3 61.2 %copy-start.17 = (bf16[1,1,352,2048]{3,2,1,0:T(8,128)(2,1)S(1)}, bf16[1,1,352,2048]{3,2,1,0:T(8,128)(2,1)}, u32[]{:S(2)}) copy-start(bf16[1,1,352,2048]{3,2,1,0:T(8,128)(2,1)} %all-gather.9.cloned.1.call-done) | copy-start | bytes 4325380
  119.6 62.9 %copy-start.6 = (bf16[1,352,2048]{2,1,0:T(8,128)(2,1)}, bf16[1,352,2048]{2,1,0:T(8,128)(2,1)S(1)}, u32[]{:S(2)}) copy-start(bf16[1,352,2048]{2,1,0:T(8,128)(2,1)S(1)} %get-tuple-element.21) | copy-start | bytes 4325380
  119.6 58.7 %copy-start.18 = (bf16[1,1,352,2048]{3,2,1,0:T(8,128)(2,1)S(1)}, bf16[1,1,352,2048]{3,2,1,0:T(8,128)(2,1)}, u32[]{:S(2)}) copy-start(bf16[1,1,352,2048]{3,2,1,0:T(8,128)(2,1)} %all-gather.11.cloned.1.call-done) | copy-start | bytes 4325380
  182.6 2.8 copy-start.10
  182.6 2.8 copy-start.12
  182.6 2.8 copy-start.19
  185.4 1.0 copy-start.25
  185.4 1.6 copy-start.14
  185.4 2.3 copy-start.16
  186.4 2.4 copy-start.27
  190.1 15.5 %copy-start.21 = (s32[1,112,2]{1,2,0:T(2,128)S(1)}, s32[1,112,2]{1,2,0:T(2,128)}, u32[]{:S(2)}) copy-start(s32[1,112,2]{1,2,0:T(2,128)} %param.18) | copy-start | bytes 2692
  190.1 65.3 %all-to-all-start.5 = ((bf16[64,4,2048]{2,1,0:T(4,128)(2,1)}), bf16[64,4,2048]{2,1,0:T(4,128)(2,1)S(1)}, u32[]{:S(2)}, u32[]{:S(2)}) async-start(bf16[64,4,2048]{2,1,0:T(4,128)(2,1)} %reshape.527), calls=%async_computation.5 | async-start | bytes 2097152 | tf_op jit(solution)/shard_map/all_to_all | solution.py:118
  260.7 1.4 copy-start.4
  267.4 61.6 %copy-start.15 = (bf16[1,352,2048]{2,1,0:T(8,128)(2,1)S(1)}, bf16[1,352,2048]{2,1,0:T(8,128)(2,1)}, u32[]{:S(2)}) copy-start(bf16[1,352,2048]{2,1,0:T(8,128)(2,1)} %get-tuple-element.25) | copy-start | bytes 4325380
  329.0 2.8 copy-start.11
  329.0 2.8 copy-start.13
  329.0 2.8 copy-start.26
  331.8 1.4 copy-start.7
  331.8 1.8 copy-start.9
  331.9 2.0 copy-start.28
  336.2 60.4 %all-to-all-start.4 = ((bf16[64,4,2048]{2,1,0:T(4,128)(2,1)}), bf16[64,4,2048]{2,1,0:T(4,128)(2,1)S(1)}, u32[]{:S(2)}, u32[]{:S(2)}) async-start(bf16[64,4,2048]{2,1,0:T(4,128)(2,1)} %reshape.525), calls=%async_computation.4 | async-start | bytes 2097152 | tf_op jit(solution)/shard_map/all_to_all | solution.py:154
  402.1 1.5 copy-start.24
  403.5 1.0 copy-start.3
  403.5 1.1 copy-start.5
  403.5 1.1 copy-start.23
  469.2 4.0 copy-start.8
  482.6 10.7 copy-start.22
  482.6 60.9 %all-to-all-start.1 = ((bf16[64,4,2048]{2,1,0:T(4,128)(2,1)}), bf16[64,4,2048]{2,1,0:T(4,128)(2,1)S(1)}, u32[]{:S(2)}, u32[]{:S(2)}) async-start(bf16[64,4,2048]{2,1,0:T(4,128)(2,1)} %reshape.518), calls=%async_computation.1 | async-start | bytes 2097152 | tf_op jit(solution)/shard_map/all_to_all | solution.py:103
  492.8 340.3 %all-reduce.7.cloned.1.call-start = ((), (), s32[]{:S(2)}) async-start(), calls=%async_computation.6 | async-start | bytes 524288 | tf_op jit(solution)/shard_map/psum | solution.py:167
  494.4 592.7 %collective-permute-start.4 = (bf16[112,2048]{1,0:T(8,128)(2,1)}, bf16[112,2048]{1,0:T(8,128)(2,1)}, u32[]{:S(2)}, u32[]{:S(2)}) collective-permute-start(bf16[112,2048]{1,0:T(8,128)(2,1)} %get-tuple-element.35), channel_id=1, source_target_pairs={{0,384},{128,0},{256,128},{384,256},{1,385},{129,1},{257,129},{385... | collective-permute-start | bytes 1376264 | tf_op jit(solution)/shard_map/ppermute | solution.py:16
  551.2 535.8 %collective-permute-start.3 = (bf16[112,2048]{1,0:T(8,128)(2,1)S(1)}, bf16[112,2048]{1,0:T(8,128)(2,1)S(1)}, u32[]{:S(2)}, u32[]{:S(2)}) collective-permute-start(bf16[112,2048]{1,0:T(8,128)(2,1)S(1)} %fusion.21), channel_id=1, source_target_pairs={{0,128},{128,256},{256,384},{384,0},{1,129},{129,257},{257,385},{3... | collective-permute-start | bytes 1376264 | tf_op jit(solution)/shard_map/ppermute | solution.py:16
Sparse Core Ops, SparseCore 0:
  10.1 26.8 all-gather.6
  39.1 21.3 all-gather.8
  62.6 21.3 all-gather.10
  497.4 335.7 all-reduce.6
where the time goes:
time: 1100 us
  waiting for transfers between devices  549 us (50%)
  blocking collectives  372 us (34%)
  starting transfers between devices  69.6 us (6%)
  local copies, waits for them, and re-layouts  42.3 us (4%)
  other arithmetic  25.2 us (2%)
  matrix products  23.5 us (2%)
  between operations  14.8 us (1%)
    psum x1, waiting for transfers between devices, body(): router_sum, gain_sum = lax.psum((router_term, gain_term), ('expert', 'dp'))  279 us
    psum x1, blocking collectives, body(): router_sum, gain_sum = lax.psum((router_term, gain_term), ('expert', 'dp'))  252 us
    ppermute x3, waiting for transfers between devices, partner_2(): lax.ppermute(shard, axis, [(i, i ^ 1 << stride) for i in range(lax.axis_s...  85.8 us
    all_to_all x1, blocking collectives, body(): lax.all_to_all(send_grads, 'expert', split_axis=0, concat_axis=0, tiled=T...  60.5 us
    all_to_all x1, blocking collectives, body(): lax.all_to_all(send_rows, 'expert', split_axis=0, concat_axis=0, tiled=True)  60.2 us
    all_to_all x1, waiting for transfers between devices, body(): lax.all_to_all(expert_out, 'expert', split_axis=0, concat_axis=0, tiled=T...  49.7 us
    all_to_all x1, waiting for transfers between devices, body(): lax.all_to_all(grad_normed_rows, 'expert', split_axis=0, concat_axis=0, t...  48.8 us
    all_to_all x1, waiting for transfers between devices, body(): lax.all_to_all(output, 'expert', split_axis=0, concat_axis=0, tiled=True)  44.7 us
  transfers between devices with their start and end apart: 13, of which 9 were waited for; matrix products, arithmetic and copies ran while one was open for 3% of the time, Pallas kernels for 0%

commit v1 on v0

--- a/solution.py
+++ b/solution.py
@@ -164,7 +164,7 @@
     )
     router_term = jnp.einsum("te,td->ed", dlogits, normed, preferred_element_type=jnp.float32)
     gain_term = jnp.sum(dnormed * x_float * inv_rms, 0)
-    router_sum, gain_sum = lax.psum((router_term, gain_term), ("expert", "dp"))
+    router_sum, gain_sum = lax.psum(lax.psum((router_term, gain_term), "expert"), "dp")
     blocks = lax.axis_size("expert") * lax.axis_size("dp")
     dxn = dnormed * gain[None, :]
     input_grad = (

time: 1100 us -> 971 us (0.88)
  blocking collectives: 372 us -> 268 us
  waiting for transfers between devices: 549 us -> 521 us
    psum x1 -> x2, blocking collectives: 252 us -> 148 us  [the longest x1 117 us: body(): lax.psum((router_term, gain_term), 'expert')]
    all_to_all x1, waiting for transfers between devices: 44.7 us -> 0.01 us  [body(): lax.all_to_all(output, 'expert', split_axis=0, concat_axis=0, tiled=True)]
    psum x1 -> x2, waiting for transfers between devices: 279 us -> 295 us  [the longest x1 261 us: body(): lax.psum((router_term, gain_term), 'expert')]
  transfers between devices with their start and end apart: 13 -> 14, of which waited for: 9 -> 9; matrix products, arithmetic and copies ran while one was open for 3% -> 4% of each run, Pallas kernels for 0% -> 0%
where the time goes in v1:
time: 971 us; the launch traced here: 963 us
  waiting for transfers between devices  521 us (54%)
  blocking collectives  268 us (28%)
  starting transfers between devices  68.4 us (7%)
  local copies, waits for them, and re-layouts  42.4 us (4%)
  other arithmetic  25.2 us (3%)
  matrix products  23.4 us (2%)
  between operations  14.8 us (2%)
    psum x1, waiting for transfers between devices, body(): lax.psum((router_term, gain_term), 'expert')  261 us
    psum x1, blocking collectives, body(): lax.psum((router_term, gain_term), 'expert')  117 us
    ppermute x3, waiting for transfers between devices, partner_2(): lax.ppermute(shard, axis, [(i, i ^ 1 << stride) for i in range(lax.axis_s...  85.8 us
    all_to_all x1, blocking collectives, body(): lax.all_to_all(send_grads, 'expert', split_axis=0, concat_axis=0, tiled=T...  60.5 us
    all_to_all x1, blocking collectives, body(): lax.all_to_all(send_rows, 'expert', split_axis=0, concat_axis=0, tiled=True)  60.2 us
    all_to_all x1, waiting for transfers between devices, body(): lax.all_to_all(expert_out, 'expert', split_axis=0, concat_axis=0, tiled=T...  49.7 us
    all_to_all x1, waiting for transfers between devices, body(): lax.all_to_all(grad_normed_rows, 'expert', split_axis=0, concat_axis=0, t...  48.8 us
    psum x1, waiting for transfers between devices, body(): lax.psum(lax.psum((router_term, gain_term), 'expert'), 'dp')  34.7 us
  transfers between devices with their start and end apart: 14, of which 9 were waited for; matrix products, arithmetic and copies ran while one was open for 4% of the time, Pallas kernels for 0%

profile of v1, /device:TPU:1, one launch (start us, length us, event | category | flops | bytes accessed | tf_op | source)
XLA Modules:
  0.0 963.2 jit_solution(9830577875558773813)
XLA Ops:
  16.1 1.3 scatter_custom_fusion.1
  17.4 1.4 gather_fusion.3
  19.0 1.3 reshape.523
  20.2 19.3 %all-to-all-start.3 = ((bf16[64,4,2048]{2,1,0:T(4,128)(2,1)}), bf16[64,4,2048]{2,1,0:T(4,128)(2,1)S(1)}, u32[]{:S(2)}, u32[]{:S(2)}) async-start(bf16[64,4,2048]{2,1,0:T(4,128)(2,1)} %reshape.523), calls=%async_computation.3 | async-start | bytes 2097152 | tf_op jit(solution)/shard_map/all_to_all | solution.py:116
  40.3 2.9 collective-permute-start
  43.2 17.3 %all-gather.9.cloned.1.call-done = bf16[1,1,352,2048]{3,2,1,0:T(8,128)(2,1)} async-done(((bf16[1,1,176,2048]{3,2,1,0:T(8,128)(2,1)}), bf16[1,1,352,2048]{3,2,1,0:T(8,128)(2,1)}) %all-gather.9.cloned.1.call-update) | async-done | bytes 1441808 | tf_op jit(solution)/shard_map/all_gather | solution.py:70
  60.5 2.2 collective-permute-start.1
  62.7 21.4 %all-gather.11.cloned.1.call-done = bf16[1,1,352,2048]{3,2,1,0:T(8,128)(2,1)} async-done(((bf16[1,1,176,2048]{3,2,1,0:T(8,128)(2,1)}), bf16[1,1,352,2048]{3,2,1,0:T(8,128)(2,1)}) %all-gather.11.cloned.1.call-update) | async-done | bytes 1441808 | tf_op jit(solution)/shard_map/all_gather | solution.py:71
  84.1 2.2 collective-permute-start.2
  86.3 30.3 %collective-permute-done = bf16[352,2048]{1,0:T(8,128)(2,1)} collective-permute-done((bf16[352,2048]{1,0:T(8,128)(2,1)}, bf16[352,2048]{1,0:T(8,128)(2,1)}, u32[]{:S(2)}, u32[]{:S(2)}) %collective-permute-start) | collective-permute-done | bytes 1441824 | tf_op jit(solution)/shard_map/ppermute | solution.py:10
  116.6 3.1 select_bitcast_fusion.5
  119.7 27.8 %collective-permute-done.1 = bf16[352,2048]{1,0:T(8,128)(2,1)} collective-permute-done((bf16[352,2048]{1,0:T(8,128)(2,1)}, bf16[352,2048]{1,0:T(8,128)(2,1)}, u32[]{:S(2)}, u32[]{:S(2)}) %collective-permute-start.1) | collective-permute-done | bytes 1441824 | tf_op jit(solution)/shard_map/ppermute | solution.py:10
  147.5 3.2 select_bitcast_fusion.3
  150.6 27.7 %collective-permute-done.2 = bf16[352,2048]{1,0:T(8,128)(2,1)} collective-permute-done((bf16[352,2048]{1,0:T(8,128)(2,1)}, bf16[352,2048]{1,0:T(8,128)(2,1)}, u32[]{:S(2)}, u32[]{:S(2)}) %collective-permute-start.2) | collective-permute-done | bytes 1441824 | tf_op jit(solution)/shard_map/ppermute | solution.py:10
  178.4 3.1 select_bitcast_fusion.1
  182.6 2.8 fusion.45
  190.1 15.0 %all-to-all-start.5 = ((bf16[64,4,2048]{2,1,0:T(4,128)(2,1)}), bf16[64,4,2048]{2,1,0:T(4,128)(2,1)S(1)}, u32[]{:S(2)}, u32[]{:S(2)}) async-start(bf16[64,4,2048]{2,1,0:T(4,128)(2,1)} %reshape.527), calls=%async_computation.5 | async-start | bytes 2097152 | tf_op jit(solution)/shard_map/all_to_all | solution.py:118
  205.7 49.7 %all-to-all-done.5 = bf16[64,4,2048]{2,1,0:T(4,128)(2,1)S(1)} async-done(((bf16[64,4,2048]{2,1,0:T(4,128)(2,1)}), bf16[64,4,2048]{2,1,0:T(4,128)(2,1)S(1)}, u32[]{:S(2)}, u32[]{:S(2)}) %all-to-all-start.5) | async-done | bytes 1048608 | tf_op jit(solution)/shard_map/all_to_all | solution.py:118
  256.9 1.4 select_convert_fusion
  258.3 2.4 reshape.537
  260.7 1.4 fusion.96
  265.0 1.4 gather_fusion
  267.4 60.5 %all_to_all.30 = bf16[64,4,2048]{2,1,0:T(4,128)(2,1)S(1)} all-to-all(bf16[64,4,2048]{2,1,0:T(4,128)(2,1)S(1)} %broadcast_select_fusion.2), channel_id=1, replica_groups=mesh['segment'=4,'expert'=64,'dp'=2] {'expert'}, dimensions={0} | all-to-all | bytes 2097152 | tf_op jit(solution)/shard_map/all_to_all | solution.py:136
  329.0 2.8 fusion.42
  335.0 1.3 reshape.525
  336.2 10.1 %all-to-all-start.4 = ((bf16[64,4,2048]{2,1,0:T(4,128)(2,1)}), bf16[64,4,2048]{2,1,0:T(4,128)(2,1)S(1)}, u32[]{:S(2)}, u32[]{:S(2)}) async-start(bf16[64,4,2048]{2,1,0:T(4,128)(2,1)} %reshape.525), calls=%async_computation.4 | async-start | bytes 2097152 | tf_op jit(solution)/shard_map/all_to_all | solution.py:154
  346.4 1.4 scatter_custom_fusion
  347.9 48.8 %all-to-all-done.4 = bf16[64,4,2048]{2,1,0:T(4,128)(2,1)S(1)} async-done(((bf16[64,4,2048]{2,1,0:T(4,128)(2,1)}), bf16[64,4,2048]{2,1,0:T(4,128)(2,1)S(1)}, u32[]{:S(2)}, u32[]{:S(2)}) %all-to-all-start.4) | async-done | bytes 1048608 | tf_op jit(solution)/shard_map/all_to_all | solution.py:154
  398.2 1.5 select_convert_fusion.1
  399.7 2.4 reshape.536
  402.1 1.4 fusion.95
  405.9 1.4 gather_fusion.1
  407.9 60.2 %all_to_all.31 = bf16[64,4,2048]{2,1,0:T(4,128)(2,1)S(1)} all-to-all(bf16[64,4,2048]{2,1,0:T(4,128)(2,1)S(1)} %reshape.516), channel_id=1, replica_groups=mesh['segment'=4,'expert'=64,'dp'=2] {'expert'}, dimensions={0} | all-to-all | bytes 2097152 | tf_op jit(solution)/shard_map/all_to_all | solution.py:101
  469.3 4.0 fusion.44
  473.3 7.0 fusion.2
  480.4 2.2 reshape.518
  482.6 10.2 %all-to-all-start.1 = ((bf16[64,4,2048]{2,1,0:T(4,128)(2,1)}), bf16[64,4,2048]{2,1,0:T(4,128)(2,1)S(1)}, u32[]{:S(2)}, u32[]{:S(2)}) async-start(bf16[64,4,2048]{2,1,0:T(4,128)(2,1)} %reshape.518), calls=%async_computation.1 | async-start | bytes 2097152 | tf_op jit(solution)/shard_map/all_to_all | solution.py:103
  494.4 260.8 %all-reduce.8.cloned.1.call-done = f32[32,2048]{1,0:T(8,128)} async-done(((f32[32,2048]{1,0:T(8,128)}), f32[32,2048]{1,0:T(8,128)}) %all-reduce.8.cloned.1.call-update) | async-done | bytes 262160 | tf_op jit(solution)/shard_map/psum | solution.py:167
  755.3 4.3 collective-permute-start.4
  761.2 1.5 select_convert_fusion.2
  762.6 2.4 reshape.531
  765.0 1.4 fusion.97
  767.3 1.9 collective-permute-start.3
  769.3 34.7 %all-reduce.10.cloned.1.call-done = f32[32,2048]{1,0:T(8,128)} async-done(((f32[32,2048]{1,0:T(8,128)}), f32[32,2048]{1,0:T(8,128)}) %all-reduce.10.cloned.1.call-update) | async-done | bytes 262160 | tf_op jit(solution)/shard_map/psum | solution.py:167
  804.0 1.7 multiply_bitcast_fusion
  805.6 117.5 %psum.30 = f32[2048]{0:T(1024)S(1)} all-reduce(f32[2048]{0:T(1024)S(1)} %get-tuple-element.6), channel_id=1, replica_groups=mesh['segment'=4,'expert'=64,'dp'=2] {'expert'}, use_global_device_ids=true, to_apply=%region_18.21 | all-reduce | flops 2048 | bytes 16384 | tf_op jit(solution)/shard_map/psum | solution.py:167
  923.1 30.1 %psum.31 = f32[2048]{0:T(1024)S(1)} all-reduce(f32[2048]{0:T(1024)S(1)} %psum.30), channel_id=1, replica_groups=mesh['segment'=4,'expert'=64,'dp'=2] {'dp'}, use_global_device_ids=true, to_apply=%region_19.22 | all-reduce | flops 2048 | bytes 16384 | tf_op jit(solution)/shard_map/psum | solution.py:167
  954.6 1.8 copy.75
  (160 shorter events, 36.4 us)
Async XLA Ops:
  7.2 198.1 %copy-start = (bf16[1,32,2048]{2,1,0:T(8,128)(2,1)S(1)}, bf16[1,32,2048]{2,1,0:T(8,128)(2,1)}, u32[]{:S(2)}) copy-start(bf16[1,32,2048]{2,1,0:T(8,128)(2,1)} %param.20) | copy-start | bytes 393220
  7.2 7.2 copy-start.2
  7.2 7.4 copy-start.1
  7.2 8.1 copy-start.20
  7.2 33.1 %all-gather.7.cloned.1.call-start = ((), (), s32[]{:S(2)}) async-start(), calls=%async_computation.8 | async-start | bytes 2162688 | tf_op jit(solution)/shard_map/all_gather | solution.py:69
  7.9 52.6 %all-gather.9.cloned.1.call-start = ((), (), s32[]{:S(2)}) async-start(), calls=%async_computation.9 | async-start | bytes 2162688 | tf_op jit(solution)/shard_map/all_gather | solution.py:70
  20.2 161.3 %all-to-all-start.3 = ((bf16[64,4,2048]{2,1,0:T(4,128)(2,1)}), bf16[64,4,2048]{2,1,0:T(4,128)(2,1)S(1)}, u32[]{:S(2)}, u32[]{:S(2)}) async-start(bf16[64,4,2048]{2,1,0:T(4,128)(2,1)} %reshape.523), calls=%async_computation.3 | async-start | bytes 2097152 | tf_op jit(solution)/shard_map/all_to_all | solution.py:116
  39.5 44.5 %all-gather.11.cloned.1.call-start = ((), (), s32[]{:S(2)}) async-start(), calls=%async_computation.10 | async-start | bytes 2162688 | tf_op jit(solution)/shard_map/all_gather | solution.py:71
  40.3 76.3 %collective-permute-start = (bf16[352,2048]{1,0:T(8,128)(2,1)}, bf16[352,2048]{1,0:T(8,128)(2,1)}, u32[]{:S(2)}, u32[]{:S(2)}) collective-permute-start(bf16[352,2048]{1,0:T(8,128)(2,1)} %bitcast.208), channel_id=1, source_target_pairs={{0,2},{2,0},{4,6},{6,4},{8,10},{10,8},{12,14},{14,12},{16,18},{18,... | collective-permute-start | bytes 4325384 | tf_op jit(solution)/shard_map/ppermute | solution.py:10
  60.5 86.9 %collective-permute-start.1 = (bf16[352,2048]{1,0:T(8,128)(2,1)}, bf16[352,2048]{1,0:T(8,128)(2,1)}, u32[]{:S(2)}, u32[]{:S(2)}) collective-permute-start(bf16[352,2048]{1,0:T(8,128)(2,1)} %bitcast.209), channel_id=1, source_target_pairs={{0,2},{2,0},{4,6},{6,4},{8,10},{10,8},{12,14},{14,12},{16,18},{18,... | collective-permute-start | bytes 4325384 | tf_op jit(solution)/shard_map/ppermute | solution.py:10
  84.1 94.3 %collective-permute-start.2 = (bf16[352,2048]{1,0:T(8,128)(2,1)}, bf16[352,2048]{1,0:T(8,128)(2,1)}, u32[]{:S(2)}, u32[]{:S(2)}) collective-permute-start(bf16[352,2048]{1,0:T(8,128)(2,1)} %bitcast.210), channel_id=1, source_target_pairs={{0,2},{2,0},{4,6},{6,4},{8,10},{10,8},{12,14},{14,12},{16,18},{18,... | collective-permute-start | bytes 4325384 | tf_op jit(solution)/shard_map/ppermute | solution.py:10
  86.3 61.2 %copy-start.17 = (bf16[1,1,352,2048]{3,2,1,0:T(8,128)(2,1)S(1)}, bf16[1,1,352,2048]{3,2,1,0:T(8,128)(2,1)}, u32[]{:S(2)}) copy-start(bf16[1,1,352,2048]{3,2,1,0:T(8,128)(2,1)} %all-gather.9.cloned.1.call-done) | copy-start | bytes 4325380
  119.7 62.9 %copy-start.6 = (bf16[1,352,2048]{2,1,0:T(8,128)(2,1)}, bf16[1,352,2048]{2,1,0:T(8,128)(2,1)S(1)}, u32[]{:S(2)}) copy-start(bf16[1,352,2048]{2,1,0:T(8,128)(2,1)S(1)} %get-tuple-element.21) | copy-start | bytes 4325380
  119.7 58.7 %copy-start.18 = (bf16[1,1,352,2048]{3,2,1,0:T(8,128)(2,1)S(1)}, bf16[1,1,352,2048]{3,2,1,0:T(8,128)(2,1)}, u32[]{:S(2)}) copy-start(bf16[1,1,352,2048]{3,2,1,0:T(8,128)(2,1)} %all-gather.11.cloned.1.call-done) | copy-start | bytes 4325380
  182.6 2.8 copy-start.10
  182.6 2.8 copy-start.12
  182.6 2.8 copy-start.19
  185.4 1.0 copy-start.25
  185.4 1.6 copy-start.14
  185.4 2.3 copy-start.16
  186.4 2.4 copy-start.27
  190.1 15.6 %copy-start.21 = (s32[1,112,2]{1,2,0:T(2,128)S(1)}, s32[1,112,2]{1,2,0:T(2,128)}, u32[]{:S(2)}) copy-start(s32[1,112,2]{1,2,0:T(2,128)} %param.18) | copy-start | bytes 2692
  190.1 65.3 %all-to-all-start.5 = ((bf16[64,4,2048]{2,1,0:T(4,128)(2,1)}), bf16[64,4,2048]{2,1,0:T(4,128)(2,1)S(1)}, u32[]{:S(2)}, u32[]{:S(2)}) async-start(bf16[64,4,2048]{2,1,0:T(4,128)(2,1)} %reshape.527), calls=%async_computation.5 | async-start | bytes 2097152 | tf_op jit(solution)/shard_map/all_to_all | solution.py:118
  260.7 1.4 copy-start.4
  267.4 61.6 %copy-start.15 = (bf16[1,352,2048]{2,1,0:T(8,128)(2,1)S(1)}, bf16[1,352,2048]{2,1,0:T(8,128)(2,1)}, u32[]{:S(2)}) copy-start(bf16[1,352,2048]{2,1,0:T(8,128)(2,1)} %get-tuple-element.25) | copy-start | bytes 4325380
  329.0 2.8 copy-start.11
  329.0 2.8 copy-start.13
  329.0 2.8 copy-start.26
  331.8 1.4 copy-start.7
  331.8 1.8 copy-start.9
  331.9 2.0 copy-start.28
  336.2 60.4 %all-to-all-start.4 = ((bf16[64,4,2048]{2,1,0:T(4,128)(2,1)}), bf16[64,4,2048]{2,1,0:T(4,128)(2,1)S(1)}, u32[]{:S(2)}, u32[]{:S(2)}) async-start(bf16[64,4,2048]{2,1,0:T(4,128)(2,1)} %reshape.525), calls=%async_computation.4 | async-start | bytes 2097152 | tf_op jit(solution)/shard_map/all_to_all | solution.py:154
  402.1 1.5 copy-start.24
  403.5 1.0 copy-start.3
  403.5 1.1 copy-start.5
  403.5 1.1 copy-start.23
  469.3 4.0 copy-start.8
  482.6 10.6 %copy-start.22 = (s32[1,112,2]{1,2,0:T(2,128)S(1)}, s32[1,112,2]{1,2,0:T(2,128)}, u32[]{:S(2)}) copy-start(s32[1,112,2]{1,2,0:T(2,128)} %param.17) | copy-start | bytes 2692
  482.6 277.0 %all-to-all-start.1 = ((bf16[64,4,2048]{2,1,0:T(4,128)(2,1)}), bf16[64,4,2048]{2,1,0:T(4,128)(2,1)S(1)}, u32[]{:S(2)}, u32[]{:S(2)}) async-start(bf16[64,4,2048]{2,1,0:T(4,128)(2,1)} %reshape.518), calls=%async_computation.1 | async-start | bytes 2097152 | tf_op jit(solution)/shard_map/all_to_all | solution.py:103
  492.8 262.4 %all-reduce.8.cloned.1.call-start = ((), (), s32[]{:S(2)}) async-start(), calls=%async_computation.6 | async-start | bytes 524288 | tf_op jit(solution)/shard_map/psum | solution.py:167
  494.4 309.6 %all-reduce.10.cloned.1.call-start = ((), (), s32[]{:S(2)}) async-start(), calls=%async_computation.7 | async-start | bytes 524288 | tf_op jit(solution)/shard_map/psum | solution.py:167
  755.3 198.5 %collective-permute-start.4 = (bf16[112,2048]{1,0:T(8,128)(2,1)}, bf16[112,2048]{1,0:T(8,128)(2,1)}, u32[]{:S(2)}, u32[]{:S(2)}) collective-permute-start(bf16[112,2048]{1,0:T(8,128)(2,1)} %get-tuple-element.35), channel_id=1, source_target_pairs={{0,384},{128,0},{256,128},{384,256},{1,385},{129,1},{257,129},{385... | collective-permute-start | bytes 1376264 | tf_op jit(solution)/shard_map/ppermute | solution.py:16
  767.3 186.5 %collective-permute-start.3 = (bf16[112,2048]{1,0:T(8,128)(2,1)S(1)}, bf16[112,2048]{1,0:T(8,128)(2,1)S(1)}, u32[]{:S(2)}, u32[]{:S(2)}) collective-permute-start(bf16[112,2048]{1,0:T(8,128)(2,1)S(1)} %fusion.21), channel_id=1, source_target_pairs={{0,128},{128,256},{256,384},{384,0},{1,129},{129,257},{257,385},{3... | collective-permute-start | bytes 1376264 | tf_op jit(solution)/shard_map/ppermute | solution.py:16
Sparse Core Ops, SparseCore 0:
  10.1 26.8 all-gather.6
  39.1 21.3 all-gather.8
  62.6 21.3 all-gather.10
  497.4 257.8 all-reduce.7
  758.2 45.7 all-reduce.9
